TPU v7x, 256 devices: a whole 4x4x8 slice. The times are simulated.
256 devices in a mesh: rows: 64 (over z_hi, y, x, core), ch: 4 (over z_lo).
Axes of the slice: x: 4, y: 4, z: 8 (z_hi: 2, z_lo: 4; z = z_hi * 4 + z_lo), core: 2. Of those that a mesh axis runs over, the one named last changes fastest.
Arguments:
- pixels: bfloat16 [256, 96, 2048], P('rows', 'ch'), may hold values from -6 to 6
- depth_weight: float32 [96, 9], P('ch'), may hold values from -2 to 2
- mix_weight: bfloat16 [96, 96], replicated, may hold values from -0.625 to 0.625
- spectral_real: bfloat16 [256, 96, 1024], P(None, 'ch', 'rows'), may hold values from -4 to 4
- spectral_imag: bfloat16 [256, 96, 1024], P(None, 'ch', 'rows'), may hold values from -4 to 4
- query_weight: bfloat16 [96, 128], P('ch'), may hold values from -0.625 to 0.625
- key_weight: bfloat16 [96, 128], P('ch'), may hold values from -0.625 to 0.625
- query_pixels: int32 [4096], P('rows'), may hold values from 0 to 8191
- key_pixels: int32 [16384], P('rows'), may hold values from 0 to 8191
- positives: int32 [4096], P('rows'), may hold values from 0 to 16383
Outputs:
- encoded: bfloat16 [256, 96, 2048], P('rows', 'ch')
- losses: float32 [4096], P(('rows', 'ch'))
Inputs may be any that keep to these rules, and one draw needn't show every extreme that they name: `query_pixels`: each entry is r * 2048 + x for a pixel at row r and column x of the query's own slab of 4 rows. `key_pixels`: each entry is r * 2048 + x for a pixel at row r and column x of the key's own slab of 4 rows. `positives`: the number of the positive key among all 16384 keys, numbered slab by slab in the order of key_pixels.
All inputs are finite; a program needn't handle non-finite values.
Results may differ from a plain program's by a relative error of at most 0.0065.
Values may be sent and summed in bfloat16 or wider, within the bound.
A program may use at most 64 MiB of HBM per device.

v0:
```python
import jax
import jax.numpy as jnp
from jax import lax
from jax.sharding import PartitionSpec as P

DILATION = 2


score_scale = 10.0
exact = lax.Precision.HIGHEST


def extended(cells, sides, width):
    for axis, dim in sides:
        count = lax.axis_size(axis)
        ends = count - 1
        head = lax.slice_in_dim(cells, 0, width, axis=dim)
        tail = lax.slice_in_dim(cells, cells.shape[dim] - width, cells.shape[dim], axis=dim)
        cells = jnp.concatenate(
            [
                lax.ppermute(tail, axis, [(i, (i + 1) % count) for i in range(ends)]),
                cells,
                lax.ppermute(head, axis, [((i + 1) % count, i) for i in range(ends)]),
            ],
            axis=dim,
        )
    return cells


def unit_rows(values):
    return values * lax.rsqrt(jnp.sum(values * values, axis=1, keepdims=True) + 1e-06)


def angle_table(left_len, right_len, length, direction):
    left_index = lax.broadcasted_iota(jnp.int32, (left_len, right_len), 0)
    right_index = lax.broadcasted_iota(jnp.int32, (left_len, right_len), 1)
    phase_turns = left_index * right_index % length
    angles = phase_turns.astype(jnp.float32) * (direction * 2.0 * jnp.pi / length)
    return (jnp.cos(angles), jnp.sin(angles))


def transform_last(real_part, imag_part, direction, real_only, lower_half):
    length = real_part.shape[-1]
    first_len = 1 << (length.bit_length() - 1) // 2
    second = length // first_len
    kept = second // 2 if lower_half else second
    leading = real_part.shape[:-1]
    cos_first, sin_first = angle_table(first_len, first_len, first_len, direction)
    cos_twist, sin_twist = angle_table(first_len, second, length, direction)
    cos_second, sin_second = angle_table(second, second, second, direction)
    cos_second = cos_second[:, :kept]
    sin_second = sin_second[:, :kept]

    def over_first(matrix, values):
        return jnp.einsum("ka,...ab->...kb", matrix, values, precision=exact)

    def over_second(values, matrix):
        return jnp.einsum("...kb,bm->...km", values, matrix, precision=exact)

    real_grid = real_part.reshape(leading + (first_len, second))
    if imag_part is None:
        segment_real = over_first(cos_first, real_grid)
        segment_imag = over_first(sin_first, real_grid)
    else:
        imag_grid = imag_part.reshape(leading + (first_len, second))
        segment_real = over_first(cos_first, real_grid) - over_first(sin_first, imag_grid)
        segment_imag = over_first(sin_first, real_grid) + over_first(cos_first, imag_grid)
    twisted_real = segment_real * cos_twist - segment_imag * sin_twist
    twisted_imag = segment_real * sin_twist + segment_imag * cos_twist
    result_real = over_second(twisted_real, cos_second) - over_second(twisted_imag, sin_second)
    result_real = jnp.swapaxes(result_real, -1, -2).reshape(leading + (kept * first_len,))
    if real_only:
        return result_real
    result_imag = over_second(twisted_real, sin_second) + over_second(twisted_imag, cos_second)
    result_imag = jnp.swapaxes(result_imag, -1, -2).reshape(leading + (kept * first_len,))
    return (result_real, result_imag)


def transform_first(real_part, imag_part, direction):
    moved_real = jnp.moveaxis(real_part, 0, -1)
    moved_imag = jnp.moveaxis(imag_part, 0, -1)
    result_real, result_imag = transform_last(moved_real, moved_imag, direction, False, False)
    return (jnp.moveaxis(result_real, -1, 0), jnp.moveaxis(result_imag, -1, 0))


def score_fold(query_unit, targets, key_number):

    def add_block(carried, shard_piece, offset):
        scores = (
            jnp.einsum("qd,kd->qk", query_unit, shard_piece, preferred_element_type=jnp.float32)
            * score_scale
        )
        numbers = key_number(lax.broadcasted_iota(jnp.int32, (1, shard_piece.shape[0]), 1))
        exp_sums = jnp.sum(jnp.exp(scores), axis=1)
        picked = jnp.sum(jnp.where(targets[:, None] == numbers, scores, 0.0), axis=1)
        return (exp_sums, picked)

    return add_block


def same_number(gathered):
    return gathered


def body(
    pixels,
    depth_weight,
    mix_weight,
    spectral_real,
    spectral_imag,
    query_weight,
    key_weight,
    query_pixels,
    key_pixels,
    positives,
):
    slab_rows, groups, columns = pixels.shape
    half_cols = columns // 2
    channel = lax.axis_index("ch")
    group_count = lax.axis_size("ch")
    padded = extended(pixels, (("rows", 0),), DILATION)
    padded = jnp.pad(padded, ((0, 0), (0, 0), (DILATION, DILATION)))
    summed = pixels.astype(jnp.float32)
    for tap_row in range(3):
        for tap_col in range(3):
            shifted = padded[
                tap_row * DILATION : tap_row * DILATION + slab_rows,
                :,
                tap_col * DILATION : tap_col * DILATION + columns,
            ]
            summed = summed + depth_weight[:, 3 * tap_row + tap_col][
                None, :, None
            ] * shifted.astype(jnp.float32)
    conv_out = summed.astype(jnp.bfloat16)
    local_columns = lax.dynamic_slice_in_dim(mix_weight, channel * groups, groups, 1)
    mixture = jnp.einsum(
        "rcw,cd->rdw",
        lax.all_gather(conv_out, "ch", axis=1, tiled=True),
        local_columns,
        preferred_element_type=jnp.float32,
    )
    hidden = jax.nn.gelu(mixture).astype(jnp.bfloat16)
    spectrum_real, spectrum_imag = transform_last(
        hidden.astype(jnp.float32), None, -1.0, False, True
    )
    column_real, column_imag = (
        lax.all_to_all(
            spectrum_real.astype(jnp.bfloat16), "rows", split_axis=2, concat_axis=0, tiled=True
        ),
        lax.all_to_all(
            spectrum_imag.astype(jnp.bfloat16), "rows", split_axis=2, concat_axis=0, tiled=True
        ),
    )
    full_real, full_imag = transform_first(
        column_real.astype(jnp.float32), column_imag.astype(jnp.float32), -1.0
    )
    kernel_real = spectral_real.astype(jnp.float32)
    kernel_imag = spectral_imag.astype(jnp.float32)
    product_real = full_real * kernel_real - full_imag * kernel_imag
    product_imag = full_real * kernel_imag + full_imag * kernel_real
    back_real, back_imag = transform_first(product_real, product_imag, 1.0)
    height = column_real.shape[0]
    back_real = (back_real * (1.0 / height)).astype(jnp.bfloat16)
    back_imag = (back_imag * (1.0 / height)).astype(jnp.bfloat16)
    row_real, row_imag = (
        lax.all_to_all(back_real, "rows", split_axis=0, concat_axis=2, tiled=True),
        lax.all_to_all(back_imag, "rows", split_axis=0, concat_axis=2, tiled=True),
    )
    doubling = jnp.where(lax.broadcasted_iota(jnp.int32, (1, 1, half_cols), 2) == 0, 1.0, 2.0)
    wide_real = jnp.pad(
        row_real.astype(jnp.float32) * doubling, ((0, 0), (0, 0), (0, columns - half_cols))
    )
    wide_imag = jnp.pad(
        row_imag.astype(jnp.float32) * doubling, ((0, 0), (0, 0), (0, columns - half_cols))
    )
    spatial = transform_last(wide_real, wide_imag, 1.0, True, False) * (1.0 / columns)
    encoded = (hidden.astype(jnp.float32) + spatial).astype(jnp.bfloat16)
    query_count = query_pixels.shape[0]
    key_features = encoded[key_pixels // columns, :, key_pixels % columns]
    key_partial = jnp.dot(key_features, key_weight, preferred_element_type=jnp.float32)
    query_features = encoded[query_pixels // columns, :, query_pixels % columns]
    query_partial = jnp.dot(query_features, query_weight, preferred_element_type=jnp.float32)
    quarter = query_count // group_count
    key_unit = unit_rows(
        lax.psum(key_partial.astype(jnp.bfloat16), "ch").astype(jnp.float32)
    ).astype(jnp.bfloat16)
    query_unit = unit_rows(
        lax.psum_scatter(
            query_partial.astype(jnp.bfloat16), "ch", scatter_dimension=0, tiled=True
        ).astype(jnp.float32)
    ).astype(jnp.bfloat16)
    targets = lax.dynamic_slice_in_dim(positives, channel * quarter, quarter, 0)
    add_block = score_fold(query_unit, targets, same_number)
    starting = (jnp.zeros((quarter,), jnp.float32), jnp.zeros((quarter,), jnp.float32))
    exp_sums, picked = add_block(
        starting, lax.all_gather(key_unit, "rows", axis=0, tiled=True), jnp.int32(0)
    )
    losses = jnp.log(exp_sums) - picked
    return (encoded, losses)


def solution(mesh):
    placed = (
        P("rows", "ch", None),
        P("ch", None),
        P(),
        P(None, "ch", "rows"),
        P(None, "ch", "rows"),
        P("ch", None),
        P("ch", None),
        P("rows"),
        P("rows"),
        P("rows"),
    )
    return jax.shard_map(
        body,
        mesh=mesh,
        in_specs=placed,
        out_specs=(P("rows", "ch", None), P(("rows", "ch"))),
        check_vma=False,
    )
```

profile of v0, /device:TPU:1, one launch (start us, length us, event | category | flops | bytes accessed | tf_op | source)
XLA Modules:
  0.0 488.4 jit_solution(1432009338411808020)
XLA Ops:
  8.3 4.5 collective-permute-start
  15.8 4.1 collective-permute-done.1
  23.4 52.8 %all-gather.3.cloned.1.call-done = bf16[4,96,2048]{2,1,0:T(8,128)(2,1)} async-done(((bf16[4,24,2048]{2,1,0:T(8,128)(2,1)}), bf16[4,96,2048]{2,1,0:T(8,128)(2,1)}) %all-gather.3.cloned.1.call-update) | async-done | bytes 1572880 | tf_op jit(solution)/shard_map/all_gather | solution.py:138
  84.3 2.4 fusion.45
  86.7 3.8 copy.200
  90.5 4.1 reshape.227
  94.6 11.6 %all-to-all-start = ((bf16[64,2,768]{2,1,0:T(2,128)(2,1)}), bf16[64,2,768]{2,1,0:T(2,128)(2,1)S(1)}, u32[]{:S(2)}, u32[]{:S(2)}) async-start(bf16[64,2,768]{2,1,0:T(2,128)(2,1)} %reshape.227), calls=%async_computation | async-start | bytes 393216 | tf_op jit(solution)/shard_map/all_to_all | solution.py:147
  107.7 2.5 fusion.46
  110.2 3.1 copy.206
  115.5 3.8 all-to-all-done
  119.2 9.2 %all-to-all-start.1 = ((bf16[64,2,768]{2,1,0:T(2,128)(2,1)}), bf16[64,2,768]{2,1,0:T(2,128)(2,1)}, u32[]{:S(2)}, u32[]{:S(2)}) async-start(bf16[64,2,768]{2,1,0:T(2,128)(2,1)} %reshape.229), calls=%async_computation.1 | async-start | bytes 393216 | tf_op jit(solution)/shard_map/all_to_all | solution.py:150
  130.2 3.2 fusion.52
  135.4 6.0 %all-to-all-done.1 = bf16[64,2,768]{2,1,0:T(2,128)(2,1)} async-done(((bf16[64,2,768]{2,1,0:T(2,128)(2,1)}), bf16[64,2,768]{2,1,0:T(2,128)(2,1)}, u32[]{:S(2)}, u32[]{:S(2)}) %all-to-all-start.1) | async-done | bytes 196640 | tf_op jit(solution)/shard_map/all_to_all | solution.py:150
  141.4 12.7 %reshape.230 = bf16[1024,4,24]{2,1,0:T(4,128)(2,1)S(1)} reshape(bf16[64,2,768]{2,1,0:T(2,128)(2,1)} %all-to-all-done.1) | data formatting | bytes 393216
  156.4 2.5 fusion.2
  158.9 2.4 fusion.12
  163.8 4.3 subtract_bitcast_fusion
  168.1 3.9 add_bitcast_fusion
  171.9 3.8 copy.156
  177.9 3.8 copy.153
  185.1 2.6 reshape.162
  187.8 3.4 copy.157
  191.2 3.3 fusion.142
  194.5 3.3 fusion.148
  197.8 2.6 reshape.163
  200.4 3.6 copy.159
  204.0 3.7 convolution_subtract_fusion
  207.7 2.4 fusion
  212.6 2.6 fusion.39
  215.2 3.5 copy.167
  218.7 3.2 convert_element_type.291
  225.1 6.8 %all-to-all-start.2 = ((bf16[64,2,768]{2,1,0:T(2,128)(2,1)}), bf16[64,2,768]{2,1,0:T(2,128)(2,1)S(1)}, u32[]{:S(2)}, u32[]{:S(2)}) async-start(bf16[64,2,768]{2,1,0:T(2,128)(2,1)} %reshape.231), calls=%async_computation.2 | async-start | bytes 393216 | tf_op jit(solution)/shard_map/all_to_all | solution.py:166
  231.9 2.4 fusion.4
  234.3 2.6 fusion.42
  236.9 2.7 copy.172
  244.9 12.3 %all-to-all-start.3 = ((bf16[64,2,768]{2,1,0:T(2,128)(2,1)}), bf16[64,2,768]{2,1,0:T(2,128)(2,1)S(1)}, u32[]{:S(2)}, u32[]{:S(2)}) async-start(bf16[64,2,768]{2,1,0:T(2,128)(2,1)} %reshape.233), calls=%async_computation.3 | async-start | bytes 393216 | tf_op jit(solution)/shard_map/all_to_all | solution.py:167
  260.5 3.9 copy.169
  264.5 3.3 reshape.166
  267.7 2.5 all-to-all-done.3
  273.3 3.9 copy.174
  277.2 3.3 reshape.167
  283.1 2.7 fusion.115
  290.4 3.0 convolution_add_fusion.2
  296.7 2.8 multiply_bitcast_fusion
  310.5 44.3 %all-reduce.5.cloned.1.call-done = bf16[256,128]{1,0:T(8,128)(2,1)} async-done(((bf16[256,128]{1,0:T(8,128)(2,1)}), bf16[256,128]{1,0:T(8,128)(2,1)}) %all-reduce.5.cloned.1.call-update) | async-done | bytes 65552 | tf_op jit(solution)/shard_map/psum | solution.py:185
  357.5 22.7 %reduce-scatter.2.cloned.1.call-done = bf16[16,128]{1,0:T(8,128)(2,1)} async-done(((bf16[64,128]{1,0:T(8,128)(2,1)}), bf16[16,128]{1,0:T(8,128)(2,1)}) %reduce-scatter.2.cloned.1.call-update) | async-done | bytes 4112 | tf_op jit(solution)/shard_map/reduce_scatter | solution.py:188
  381.0 96.5 %all-gather.5.cloned.1.call-done = bf16[16384,128]{1,0:T(8,128)(2,1)} async-done(((bf16[256,128]{1,0:T(8,128)(2,1)}), bf16[16384,128]{1,0:T(8,128)(2,1)}) %all-gather.5.cloned.1.call-update) | async-done | bytes 4194320 | tf_op jit(solution)/shard_map/all_gather | solution.py:196
  477.4 3.6 exponential_reduce_fusion
  (110 shorter events, 75.6 us)
Async XLA Ops:
  7.2 69.0 %copy-start = (bf16[96,96]{1,0:T(8,128)(2,1)S(1)}, bf16[96,96]{1,0:T(8,128)(2,1)}, u32[]{:S(2)}) copy-start(bf16[96,96]{1,0:T(8,128)(2,1)} %param.12) | copy-start | bytes 55300
  7.2 14.0 %copy-start.9 = (bf16[4,24,2048]{2,1,0:T(8,128)(2,1)S(1)}, bf16[4,24,2048]{2,1,0:T(8,128)(2,1)}, u32[]{:S(2)}) copy-start(bf16[4,24,2048]{2,1,0:T(8,128)(2,1)} %param.10) | copy-start | bytes 1179652
  7.2 69.0 %all-gather.3.cloned.1.call-start = ((), (), s32[]{:S(2)}) async-start(), calls=%async_computation.5 | async-start | bytes 1966080 | tf_op jit(solution)/shard_map/all_gather | solution.py:138
  8.3 7.4 %collective-permute-start = (bf16[2,24,2048]{2,1,0:T(8,128)(2,1)S(1)}, bf16[2,24,2048]{2,1,0:T(8,128)(2,1)S(1)}, u32[]{:S(2)}, u32[]{:S(2)}) collective-permute-start(bf16[2,24,2048]{2,1,0:T(8,128)(2,1)S(1)} %get-tuple-element.10), channel_id=1, source_target_pairs={{0,4},{4,8},{8,12},{12,16},{16,20},{20,24},{24,28},{28,32},{32,36}... | collective-permute-start | bytes 589832 | tf_op jit(solution)/shard_map/ppermute | solution.py:21
  12.8 7.0 %collective-permute-start.1 = (bf16[2,24,2048]{2,1,0:T(8,128)(2,1)S(1)}, bf16[2,24,2048]{2,1,0:T(8,128)(2,1)S(1)}, u32[]{:S(2)}, u32[]{:S(2)}) collective-permute-start(bf16[2,24,2048]{2,1,0:T(8,128)(2,1)S(1)} %get-tuple-element.11), channel_id=1, source_target_pairs={{4,0},{8,4},{12,8},{16,12},{20,16},{24,20},{28,24},{32,28},{36,32}... | collective-permute-start | bytes 589832 | tf_op jit(solution)/shard_map/ppermute | solution.py:23
  21.2 2.2 copy-start.17
  21.2 2.2 copy-start.16
  78.2 0.8 copy-start.11
  79.0 0.9 copy-start.8
  94.6 24.6 %all-to-all-start = ((bf16[64,2,768]{2,1,0:T(2,128)(2,1)}), bf16[64,2,768]{2,1,0:T(2,128)(2,1)S(1)}, u32[]{:S(2)}, u32[]{:S(2)}) async-start(bf16[64,2,768]{2,1,0:T(2,128)(2,1)} %reshape.227), calls=%async_computation | async-start | bytes 393216 | tf_op jit(solution)/shard_map/all_to_all | solution.py:147
  119.2 22.2 %all-to-all-start.1 = ((bf16[64,2,768]{2,1,0:T(2,128)(2,1)}), bf16[64,2,768]{2,1,0:T(2,128)(2,1)}, u32[]{:S(2)}, u32[]{:S(2)}) async-start(bf16[64,2,768]{2,1,0:T(2,128)(2,1)} %reshape.229), calls=%async_computation.1 | async-start | bytes 393216 | tf_op jit(solution)/shard_map/all_to_all | solution.py:150
  154.3 2.0 copy-start.7
  181.7 2.1 copy-start.13
  204.0 3.7 copy-start.6
  210.2 2.5 copy-start.4
  210.2 2.5 copy-start.2
  218.7 13.2 %copy-start.5 = (f32[24,16,16,16]{0,2,3,1:T(8,128)S(1)}, f32[24,16,16,16]{0,2,3,1:T(8,128)}, u32[]{:S(2)}) copy-start(f32[24,16,16,16]{0,2,3,1:T(8,128)} %copy-done.4) | copy-start | bytes 1179652
  225.1 19.8 %all-to-all-start.2 = ((bf16[64,2,768]{2,1,0:T(2,128)(2,1)}), bf16[64,2,768]{2,1,0:T(2,128)(2,1)S(1)}, u32[]{:S(2)}, u32[]{:S(2)}) async-start(bf16[64,2,768]{2,1,0:T(2,128)(2,1)} %reshape.231), calls=%async_computation.2 | async-start | bytes 393216 | tf_op jit(solution)/shard_map/all_to_all | solution.py:166
  231.9 2.5 copy-start.3
  244.9 25.3 %all-to-all-start.3 = ((bf16[64,2,768]{2,1,0:T(2,128)(2,1)}), bf16[64,2,768]{2,1,0:T(2,128)(2,1)S(1)}, u32[]{:S(2)}, u32[]{:S(2)}) async-start(bf16[64,2,768]{2,1,0:T(2,128)(2,1)} %reshape.233), calls=%async_computation.3 | async-start | bytes 393216 | tf_op jit(solution)/shard_map/all_to_all | solution.py:167
  257.2 97.6 %all-reduce.5.cloned.1.call-start = ((), (), s32[]{:S(2)}) async-start(), calls=%async_computation.7 | async-start | bytes 131072 | tf_op jit(solution)/shard_map/psum | solution.py:185
  285.8 1.6 copy-start.12
  304.0 4.9 %copy-start.14 = (bf16[24,128]{1,0:T(8,128)(2,1)S(1)}, bf16[24,128]{1,0:T(8,128)(2,1)}, u32[]{:S(2)}) copy-start(bf16[24,128]{1,0:T(8,128)(2,1)} %param.16) | copy-start | bytes 18436
  305.3 175.7 %copy-start.10 = (bf16[4,24,2048]{2,1,0:T(8,128)(2,1)}, bf16[4,24,2048]{2,1,0:T(8,128)(2,1)S(1)}, u32[]{:S(2)}) copy-start(bf16[4,24,2048]{2,1,0:T(8,128)(2,1)S(1)} %add_convert_fusion.1) | copy-start | bytes 1179652
  305.3 4.4 copy-start.15
  305.3 52.1 %copy-start.18 = (s32[64]{0:T(128)S(1)}, s32[64]{0:T(128)}, u32[]{:S(2)}) copy-start(s32[64]{0:T(128)} %param.19) | copy-start | bytes 772
  309.7 70.5 %reduce-scatter.2.cloned.1.call-start = ((), (), s32[]{:S(2)}) async-start(), calls=%async_computation.6 | async-start | bytes 20480 | tf_op jit(solution)/shard_map/reduce_scatter | solution.py:188
  310.5 167.0 %all-gather.5.cloned.1.call-start = ((), (), s32[]{:S(2)}) async-start(), calls=%async_computation.8 | async-start | bytes 4259840 | tf_op jit(solution)/shard_map/all_gather | solution.py:196
  381.0 100.6 %copy-start.1 = (bf16[96,96]{1,0:T(8,128)(2,1)S(1)}, bf16[96,96]{1,0:T(8,128)(2,1)}, u32[]{:S(2)}) copy-start(bf16[96,96]{1,0:T(8,128)(2,1)} %param.12) | copy-start | bytes 55300
Sparse Core Ops, SparseCore 0:
  23.1 53.0 all-gather.2
  309.8 45.0 all-reduce.4
  357.3 22.7 reduce-scatter.1
  383.6 93.8 all-gather.4
where the time goes:
time: 498 us; the launch traced here: 488 us
  waiting for transfers between devices  233 us (47%)
  local copies, waits for them, and re-layouts  102 us (20%)
  matrix products  76.5 us (15%)
  starting transfers between devices  46.7 us (9%)
  other arithmetic  15.1 us (3%)
  between operations  14.9 us (3%)
    all_gather x1, waiting for transfers between devices, body(): lax.all_gather(key_unit, 'rows', axis=0, tiled=True)  96.5 us
    all_gather x1, waiting for transfers between devices, body(): lax.all_gather(conv_out, 'ch', axis=1, tiled=True)  52.8 us
    psum x1, waiting for transfers between devices, body(): lax.psum(key_partial.astype(jnp.bfloat16), 'ch').astype(jnp.float32)  44.3 us
    dot_general x14, matrix products, over_second(): return jnp.einsum('...kb,bm->...km', values, matrix, precision=exact)  35.3 us
    dot_general x14, matrix products, over_first(): return jnp.einsum('ka,...ab->...kb', matrix, values, precision=exact)  34.2 us
    unnamed x46, local copies, waits for them, and re-layouts  28.7 us
    reduce_scatter x1, waiting for transfers between devices, body(): lax.psum_scatter(query_partial.astype(jnp.bfloat16), 'ch', scatter_dimens...  22.7 us
    all_to_all x1, starting transfers between devices, body(): lax.all_to_all(back_imag, 'rows', split_axis=0, concat_axis=2, tiled=True)  12.3 us
  transfers between devices with their start and end apart: 10, of which 9 were waited for; matrix products, arithmetic and copies ran while one was open for 9% of the time, Pallas kernels for 0%

commit v1 on v0

--- a/solution.py
+++ b/solution.py
@@ -143,14 +143,9 @@
     spectrum_real, spectrum_imag = transform_last(
         hidden.astype(jnp.float32), None, -1.0, False, True
     )
-    column_real, column_imag = (
-        lax.all_to_all(
-            spectrum_real.astype(jnp.bfloat16), "rows", split_axis=2, concat_axis=0, tiled=True
-        ),
-        lax.all_to_all(
-            spectrum_imag.astype(jnp.bfloat16), "rows", split_axis=2, concat_axis=0, tiled=True
-        ),
-    )
+    wire = jnp.stack([spectrum_real, spectrum_imag]).astype(jnp.bfloat16)
+    columns_both = lax.all_to_all(wire, "rows", split_axis=3, concat_axis=1, tiled=True)
+    column_real, column_imag = columns_both[0], columns_both[1]
     full_real, full_imag = transform_first(
         column_real.astype(jnp.float32), column_imag.astype(jnp.float32), -1.0
     )
@@ -162,10 +157,10 @@
     height = column_real.shape[0]
     back_real = (back_real * (1.0 / height)).astype(jnp.bfloat16)
     back_imag = (back_imag * (1.0 / height)).astype(jnp.bfloat16)
-    row_real, row_imag = (
-        lax.all_to_all(back_real, "rows", split_axis=0, concat_axis=2, tiled=True),
-        lax.all_to_all(back_imag, "rows", split_axis=0, concat_axis=2, tiled=True),
-    )
+    rows_both = lax.all_to_all(
+        jnp.stack([back_real, back_imag]), "rows", split_axis=1, concat_axis=3, tiled=True
+    )
+    row_real, row_imag = rows_both[0], rows_both[1]
     doubling = jnp.where(lax.broadcasted_iota(jnp.int32, (1, 1, half_cols), 2) == 0, 1.0, 2.0)
     wide_real = jnp.pad(
         row_real.astype(jnp.float32) * doubling, ((0, 0), (0, 0), (0, columns - half_cols))
@@ -175,27 +170,43 @@
     )
     spatial = transform_last(wide_real, wide_imag, 1.0, True, False) * (1.0 / columns)
     encoded = (hidden.astype(jnp.float32) + spatial).astype(jnp.bfloat16)
+    key_count = key_pixels.shape[0]
     query_count = query_pixels.shape[0]
-    key_features = encoded[key_pixels // columns, :, key_pixels % columns]
-    key_partial = jnp.dot(key_features, key_weight, preferred_element_type=jnp.float32)
-    query_features = encoded[query_pixels // columns, :, query_pixels % columns]
-    query_partial = jnp.dot(query_features, query_weight, preferred_element_type=jnp.float32)
     quarter = query_count // group_count
+    slab = lax.axis_index("rows")
+    weights_all = lax.all_gather(
+        jnp.concatenate([key_weight, query_weight], axis=1), "ch", axis=0, tiled=True
+    )
+    sampled = jnp.concatenate([key_pixels, query_pixels])
+    features = encoded[sampled // columns, :, sampled % columns]
+    features = lax.all_gather(features, "ch", axis=1, tiled=True)
+    key_dim = key_weight.shape[1]
     key_unit = unit_rows(
-        lax.psum(key_partial.astype(jnp.bfloat16), "ch").astype(jnp.float32)
+        jnp.dot(features[:key_count], weights_all[:, :key_dim], preferred_element_type=jnp.float32)
     ).astype(jnp.bfloat16)
+    own_queries = lax.dynamic_slice_in_dim(features, key_count + channel * quarter, quarter, 0)
     query_unit = unit_rows(
-        lax.psum_scatter(
-            query_partial.astype(jnp.bfloat16), "ch", scatter_dimension=0, tiled=True
-        ).astype(jnp.float32)
+        jnp.dot(own_queries, weights_all[:, key_dim:], preferred_element_type=jnp.float32)
     ).astype(jnp.bfloat16)
     targets = lax.dynamic_slice_in_dim(positives, channel * quarter, quarter, 0)
-    add_block = score_fold(query_unit, targets, same_number)
-    starting = (jnp.zeros((quarter,), jnp.float32), jnp.zeros((quarter,), jnp.float32))
-    exp_sums, picked = add_block(
-        starting, lax.all_gather(key_unit, "rows", axis=0, tiled=True), jnp.int32(0)
-    )
-    losses = jnp.log(exp_sums) - picked
+    coded = jnp.concatenate([targets // 128, targets % 128]).astype(jnp.bfloat16)
+    coded = jnp.pad(coded, (0, key_dim - 2 * quarter))[None, :]
+    packet = jnp.concatenate([query_unit, coded], axis=0)
+    gathered = lax.all_gather(packet[None], "rows", axis=0, tiled=True)
+    all_queries = gathered[:, :quarter, :].reshape(-1, key_dim)
+    coded_all = gathered[:, quarter, :].astype(jnp.int32)
+    all_targets = (coded_all[:, :quarter] * 128 + coded_all[:, quarter : 2 * quarter]).reshape(-1)
+    scores = (
+        jnp.einsum("qd,kd->qk", all_queries, key_unit, preferred_element_type=jnp.float32)
+        * score_scale
+    )
+    numbers = slab * key_count + lax.broadcasted_iota(jnp.int32, (1, key_count), 1)
+    exp_sums = jnp.sum(jnp.exp(scores), axis=1)
+    picked = jnp.sum(jnp.where(all_targets[:, None] == numbers, scores, 0.0), axis=1)
+    reduced = lax.psum_scatter(
+        jnp.stack([exp_sums, picked], axis=1), "rows", scatter_dimension=0, tiled=True
+    )
+    losses = jnp.log(reduced[:, 0]) - reduced[:, 1]
     return (encoded, losses)
 
 

time: 498 us -> 876 us (1.76)
  the two profiles are of different devices: /device:TPU:1 before, /device:TPU:32 now
where the time goes in v1:
time: 876 us; the launch traced here: 867 us
  waiting for transfers between devices  491 us (56%)
  blocking collectives  139 us (16%)
  local copies, waits for them, and re-layouts  109 us (12%)
  matrix products  75.7 us (9%)
  starting transfers between devices  26.1 us (3%)
  between operations  14.9 us (2%)
  other arithmetic  10.4 us (1%)
    unnamed x3, waiting for transfers between devices  414 us
    all_gather x1, blocking collectives, body(): gathered = lax.all_gather(packet[None], 'rows', axis=0, tiled=True)  110 us
    all_gather x1, waiting for transfers between devices, body(): lax.all_gather(conv_out, 'ch', axis=1, tiled=True)  56.4 us
    dot_general x14, matrix products, over_second(): return jnp.einsum('...kb,bm->...km', values, matrix, precision=exact)  38.5 us
    dot_general x14, matrix products, over_first(): return jnp.einsum('ka,...ab->...kb', matrix, values, precision=exact)  34.2 us
    all_to_all x1, waiting for transfers between devices, body(): lax.all_to_all(jnp.stack([back_real, back_imag]), 'rows', split_axis=1, c...  17.5 us
  transfers between devices with their start and end apart: 6, of which 5 were waited for; matrix products, arithmetic and copies ran while one was open for 0% of the time, Pallas kernels for 0%

profile of v1, /device:TPU:32, one launch (start us, length us, event | category | flops | bytes accessed | tf_op | source)
XLA Modules:
  0.0 866.5 jit_solution(4636469104525805419)
XLA Ops:
  17.9 56.4 %all-gather.4.cloned.1.call-done = bf16[4,96,2048]{2,1,0:T(8,128)(2,1)} async-done(((bf16[4,24,2048]{2,1,0:T(8,128)(2,1)}), bf16[4,96,2048]{2,1,0:T(8,128)(2,1)}) %all-gather.4.cloned.1.call-update) | async-done | bytes 1572880 | tf_op jit(solution)/shard_map/all_gather | solution.py:138
  83.1 2.7 fusion.83
  85.7 2.4 fusion.46
  92.4 3.8 fusion.45
  100.2 3.6 reshape.434
  103.8 11.1 %all-to-all-start = ((bf16[64,2,1536]{2,1,0:T(2,128)(2,1)}), bf16[64,2,1536]{2,1,0:T(2,128)(2,1)S(1)}, u32[]{:S(2)}, u32[]{:S(2)}) async-start(bf16[64,2,1536]{2,1,0:T(2,128)(2,1)} %reshape.434), calls=%async_computation | async-start | bytes 786432 | tf_op jit(solution)/shard_map/all_to_all | solution.py:147
  115.0 16.3 %all_gather.14 = bf16[96,256]{1,0:T(8,128)(2,1)S(1)} all-gather(bf16[24,256]{1,0:T(8,128)(2,1)S(1)} %pad_maximum_fusion.4), channel_id=1, replica_groups=mesh['rows'=64,'ch'=4] {'ch'}, dimensions={0}, use_global_device_ids=true | all-gather | bytes 61440 | tf_op jit(solution)/shard_map/all_gather | solution.py:177
  132.3 3.9 reshape.435
  136.2 5.5 copy.239
  141.7 2.8 fusion.321
  144.5 3.6 copy.177
  148.2 3.2 fusion.52
  153.3 4.1 copy.181
  161.7 2.4 fusion.12
  164.2 2.4 fusion.14
  166.6 3.8 subtract_bitcast_fusion
  170.4 4.0 add_bitcast_fusion
  174.4 3.8 copy.194
  180.3 3.8 copy.191
  187.6 2.6 reshape.392
  190.2 3.4 copy.195
  193.6 3.3 fusion.145
  196.9 3.3 fusion.151
  200.2 2.6 reshape.393
  202.8 3.8 copy.197
  206.7 3.8 convolution_subtract_fusion
  210.4 2.6 fusion
  213.1 2.4 fusion.4
  215.5 2.4 fusion.6
  217.9 2.7 fusion.42
  220.7 3.6 fusion.39
  224.3 3.9 copy.205
  229.7 2.7 copy.208
  234.0 3.1 copy.209
  237.1 3.6 reshape.436
  240.6 11.9 %all-to-all-start.1 = ((bf16[64,2,1536]{2,1,0:T(2,128)(2,1)}), bf16[64,2,1536]{2,1,0:T(2,128)(2,1)S(1)}, u32[]{:S(2)}, u32[]{:S(2)}) async-start(bf16[64,2,1536]{2,1,0:T(2,128)(2,1)} %reshape.436), calls=%async_computation.1 | async-start | bytes 786432 | tf_op jit(solution)/shard_map/all_to_all | solution.py:160
  252.9 17.5 %all-to-all-done.1 = bf16[64,2,1536]{2,1,0:T(2,128)(2,1)S(1)} async-done(((bf16[64,2,1536]{2,1,0:T(2,128)(2,1)}), bf16[64,2,1536]{2,1,0:T(2,128)(2,1)S(1)}, u32[]{:S(2)}, u32[]{:S(2)}) %all-to-all-start.1) | async-done | bytes 393248 | tf_op jit(solution)/shard_map/all_to_all | solution.py:160
  270.4 3.0 reshape.437
  273.4 2.6 copy.211
  279.3 3.3 reshape.398
  285.0 3.3 reshape.397
  290.9 2.7 fusion.120
  298.1 3.0 convolution_add_fusion.2
  304.4 2.8 multiply_bitcast_fusion
  314.0 4.9 gather_fusion
  319.0 12.0 %all_gather.13 = bf16[320,96]{0,1:T(8,128)(2,1)S(1)} all-gather(bf16[320,24]{0,1:T(8,128)(2,1)S(1)} %copy.218), channel_id=1, replica_groups=mesh['rows'=64,'ch'=4] {'ch'}, dimensions={1}, use_global_device_ids=true | all-gather | bytes 76800 | tf_op jit(solution)/shard_map/all_gather | solution.py:182
  331.7 110.5 %all-gather.1 = bf16[64,17,128]{2,1,0:T(8,128)(2,1)S(1)} all-gather(bf16[1,17,128]{2,1,0:T(8,128)(2,1)S(1)} %maximum_bitcast_fusion), channel_id=2, replica_groups=mesh['rows'=64,'ch'=4] {'rows'}, dimensions={0}, use_global_device_ids=true | all-gather | bytes 282880 | tf_op jit(solution)/shard_map/all_gather | solution.py:195
  443.9 414.0 %reduce-scatter.4.cloned.1.call-done = f32[16,2]{1,0:T(8,128)} async-done(((f32[1024,2]{1,0:T(8,128)}), f32[16,2]{1,0:T(8,128)}) %reduce-scatter.4.cloned.1.call-update) | async-done | bytes 144
  (108 shorter events, 70.7 us)
Async XLA Ops:
  7.2 67.2 %copy-start = (bf16[96,96]{1,0:T(8,128)(2,1)S(1)}, bf16[96,96]{1,0:T(8,128)(2,1)}, u32[]{:S(2)}) copy-start(bf16[96,96]{1,0:T(8,128)(2,1)} %param.12) | copy-start | bytes 55300
  7.2 8.8 %copy-start.5 = (bf16[4,24,2048]{2,1,0:T(8,128)(2,1)S(1)}, bf16[4,24,2048]{2,1,0:T(8,128)(2,1)}, u32[]{:S(2)}) copy-start(bf16[4,24,2048]{2,1,0:T(8,128)(2,1)} %param.10) | copy-start | bytes 1179652
  7.2 67.1 %all-gather.4.cloned.1.call-start = ((), (), s32[]{:S(2)}) async-start(), calls=%async_computation.3 | async-start | bytes 1966080 | tf_op jit(solution)/shard_map/all_gather | solution.py:138
  8.3 4.0 collective-permute-start
  10.1 4.6 collective-permute-start.1
  76.3 0.8 copy-start.7
  77.9 0.9 copy-start.4
  100.2 14.7 %copy-start.12 = (s32[256]{0:T(256)S(1)}, s32[256]{0:T(256)}, u32[]{:S(2)}) copy-start(s32[256]{0:T(256)} %param.18) | copy-start | bytes 3076
  100.2 14.7 %copy-start.13 = (s32[64]{0:T(128)S(1)}, s32[64]{0:T(128)}, u32[]{:S(2)}) copy-start(s32[64]{0:T(128)} %param.17) | copy-start | bytes 772
  100.2 14.8 %copy-start.10 = (bf16[24,128]{1,0:T(8,128)(2,1)S(1)}, bf16[24,128]{1,0:T(8,128)(2,1)}, u32[]{:S(2)}) copy-start(bf16[24,128]{1,0:T(8,128)(2,1)} %param.15) | copy-start | bytes 18436
  100.2 14.7 %copy-start.11 = (bf16[24,128]{1,0:T(8,128)(2,1)S(1)}, bf16[24,128]{1,0:T(8,128)(2,1)}, u32[]{:S(2)}) copy-start(bf16[24,128]{1,0:T(8,128)(2,1)} %param.16) | copy-start | bytes 18436
  103.8 28.5 %all-to-all-start = ((bf16[64,2,1536]{2,1,0:T(2,128)(2,1)}), bf16[64,2,1536]{2,1,0:T(2,128)(2,1)S(1)}, u32[]{:S(2)}, u32[]{:S(2)}) async-start(bf16[64,2,1536]{2,1,0:T(2,128)(2,1)} %reshape.434), calls=%async_computation | async-start | bytes 786432 | tf_op jit(solution)/shard_map/all_to_all | solution.py:147
  157.4 2.0 copy-start.3
  184.1 2.1 copy-start.9
  206.6 3.8 copy-start.2
  237.0 15.5 %copy-start.14 = (s32[64]{0:T(128)S(1)}, s32[64]{0:T(128)}, u32[]{:S(2)}) copy-start(s32[64]{0:T(128)} %param.19) | copy-start | bytes 772
  240.6 29.8 %all-to-all-start.1 = ((bf16[64,2,1536]{2,1,0:T(2,128)(2,1)}), bf16[64,2,1536]{2,1,0:T(2,128)(2,1)S(1)}, u32[]{:S(2)}, u32[]{:S(2)}) async-start(bf16[64,2,1536]{2,1,0:T(2,128)(2,1)} %reshape.436), calls=%async_computation.1 | async-start | bytes 786432 | tf_op jit(solution)/shard_map/all_to_all | solution.py:160
  252.5 605.5 %reduce-scatter.4.cloned.1.call-start = ((), (), s32[]{:S(2)}) async-start(), calls=%async_computation.4 | async-start | bytes 532480
  293.6 1.5 copy-start.8
  313.0 129.2 %copy-start.6 = (bf16[4,24,2048]{2,1,0:T(8,128)(2,1)}, bf16[4,24,2048]{2,1,0:T(8,128)(2,1)S(1)}, u32[]{:S(2)}) copy-start(bf16[4,24,2048]{2,1,0:T(8,128)(2,1)S(1)} %add_convert_fusion.1) | copy-start | bytes 1179652
  331.6 527.9 %copy-start.1 = (bf16[96,96]{1,0:T(8,128)(2,1)S(1)}, bf16[96,96]{1,0:T(8,128)(2,1)}, u32[]{:S(2)}) copy-start(bf16[96,96]{1,0:T(8,128)(2,1)} %param.12) | copy-start | bytes 55300
Sparse Core Ops, SparseCore 0:
  17.9 56.3 all-gather.3
  444.1 413.8 reduce-scatter.3

commit v2 on v1

--- a/solution.py
+++ b/solution.py
@@ -25,6 +25,16 @@
             axis=dim,
         )
     return cells
+
+
+def ring_pieces(values, axis):
+    count = lax.axis_size(axis)
+    pieces = [values]
+    for shift in range(1, count):
+        pieces.append(
+            lax.ppermute(values, axis, [(i, (i + shift) % count) for i in range(count)])
+        )
+    return pieces
 
 
 def unit_rows(values):
@@ -133,10 +143,19 @@
             ] * shifted.astype(jnp.float32)
     conv_out = summed.astype(jnp.bfloat16)
     local_columns = lax.dynamic_slice_in_dim(mix_weight, channel * groups, groups, 1)
+    ordered_rows = jnp.concatenate(
+        [
+            lax.dynamic_slice_in_dim(
+                local_columns, (channel - shift) % group_count * groups, groups, 0
+            )
+            for shift in range(group_count)
+        ],
+        axis=0,
+    )
     mixture = jnp.einsum(
         "rcw,cd->rdw",
-        lax.all_gather(conv_out, "ch", axis=1, tiled=True),
-        local_columns,
+        jnp.concatenate(ring_pieces(conv_out, "ch"), axis=1),
+        ordered_rows,
         preferred_element_type=jnp.float32,
     )
     hidden = jax.nn.gelu(mixture).astype(jnp.bfloat16)
@@ -174,12 +193,12 @@
     query_count = query_pixels.shape[0]
     quarter = query_count // group_count
     slab = lax.axis_index("rows")
-    weights_all = lax.all_gather(
-        jnp.concatenate([key_weight, query_weight], axis=1), "ch", axis=0, tiled=True
+    weights_all = jnp.concatenate(
+        ring_pieces(jnp.concatenate([key_weight, query_weight], axis=1), "ch"), axis=0
     )
     sampled = jnp.concatenate([key_pixels, query_pixels])
     features = encoded[sampled // columns, :, sampled % columns]
-    features = lax.all_gather(features, "ch", axis=1, tiled=True)
+    features = jnp.concatenate(ring_pieces(features, "ch"), axis=1)
     key_dim = key_weight.shape[1]
     key_unit = unit_rows(
         jnp.dot(features[:key_count], weights_all[:, :key_dim], preferred_element_type=jnp.float32)
@@ -192,7 +211,14 @@
     coded = jnp.concatenate([targets // 128, targets % 128]).astype(jnp.bfloat16)
     coded = jnp.pad(coded, (0, key_dim - 2 * quarter))[None, :]
     packet = jnp.concatenate([query_unit, coded], axis=0)
-    gathered = lax.all_gather(packet[None], "rows", axis=0, tiled=True)
+    slabs = lax.axis_size("rows")
+    gathered = lax.all_to_all(
+        jnp.broadcast_to(packet[None], (slabs,) + packet.shape),
+        "rows",
+        split_axis=0,
+        concat_axis=0,
+        tiled=True,
+    )
     all_queries = gathered[:, :quarter, :].reshape(-1, key_dim)
     coded_all = gathered[:, quarter, :].astype(jnp.int32)
     all_targets = (coded_all[:, :quarter] * 128 + coded_all[:, quarter : 2 * quarter]).reshape(-1)
@@ -203,9 +229,13 @@
     numbers = slab * key_count + lax.broadcasted_iota(jnp.int32, (1, key_count), 1)
     exp_sums = jnp.sum(jnp.exp(scores), axis=1)
     picked = jnp.sum(jnp.where(all_targets[:, None] == numbers, scores, 0.0), axis=1)
-    reduced = lax.psum_scatter(
-        jnp.stack([exp_sums, picked], axis=1), "rows", scatter_dimension=0, tiled=True
-    )
+    reduced = lax.all_to_all(
+        jnp.stack([exp_sums, picked], axis=1).reshape(slabs, quarter, 2),
+        "rows",
+        split_axis=0,
+        concat_axis=0,
+        tiled=True,
+    ).sum(axis=0)
     losses = jnp.log(reduced[:, 0]) - reduced[:, 1]
     return (encoded, losses)
 

time: 876 us -> 348 us (0.40)
  the two profiles are of different devices: /device:TPU:32 before, /device:TPU:1 now
where the time goes in v2:
time: 348 us; the launch traced here: 344 us
  local copies, waits for them, and re-layouts  108 us (31%)
  waiting for transfers between devices  82.4 us (24%)
  matrix products  74.4 us (21%)
  starting transfers between devices  47.4 us (14%)
  blocking collectives  17.7 us (5%)
  other arithmetic  12.1 us (3%)
    dot_general x14, matrix products, over_second(): return jnp.einsum('...kb,bm->...km', values, matrix, precision=exact)  38.7 us
    ppermute x9, waiting for transfers between devices, ring_pieces(): lax.ppermute(values, axis, [(i, (i + shift) % count) for i in range(count)])  35.5 us
    dot_general x14, matrix products, over_first(): return jnp.einsum('ka,...ab->...kb', matrix, values, precision=exact)  34.3 us
    all_to_all x1, blocking collectives, body(): lax.all_to_all(jnp.stack([exp_sums, picked], axis=1).reshape(slabs, quart...  17.7 us
    all_to_all x1, waiting for transfers between devices, body(): lax.all_to_all(wire, 'rows', split_axis=3, concat_axis=1, tiled=True)  16.9 us
    unnamed x45, local copies, waits for them, and re-layouts  16.6 us
    all_to_all x1, waiting for transfers between devices, body(): lax.all_to_all(jnp.broadcast_to(packet[None], (slabs,) + packet.shape), '...  16.3 us
    ppermute x9, starting transfers between devices, ring_pieces(): lax.ppermute(values, axis, [(i, (i + shift) % count) for i in range(count)])  16.1 us
  transfers between devices with their start and end apart: 14, of which 8 were waited for; matrix products, arithmetic and copies ran while one was open for 15% of the time, Pallas kernels for 0%

profile of v2, /device:TPU:1, one launch (start us, length us, event | category | flops | bytes accessed | tf_op | source)
XLA Modules:
  0.0 343.7 jit_solution(11625355613601233252)
XLA Ops:
  1.7 4.5 %collective-permute-start = (bf16[2,24,2048]{2,1,0:T(8,128)(2,1)S(1)}, bf16[2,24,2048]{2,1,0:T(8,128)(2,1)S(1)}, u32[]{:S(2)}, u32[]{:S(2)}) collective-permute-start(bf16[2,24,2048]{2,1,0:T(8,128)(2,1)S(1)} %get-tuple-element.16), channel_id=1, source_target_pairs={{0,4},{4,8},{8,12},{12,16},{16,20},{20,24},{24,28},{28,32},{32,36}... | collective-permute-start | bytes 589832 | tf_op jit(solution)/shard_map/ppermute | solution.py:21
  9.2 4.1 %collective-permute-done.1 = bf16[2,24,2048]{2,1,0:T(8,128)(2,1)S(1)} collective-permute-done((bf16[2,24,2048]{2,1,0:T(8,128)(2,1)S(1)}, bf16[2,24,2048]{2,1,0:T(8,128)(2,1)S(1)}, u32[]{:S(2)}, u32[]{:S(2)}) %collective-permute-start.1) | collective-permute-done | bytes 196640 | tf_op jit(solution)/shard_map/ppermute | solution.py:23
  15.6 4.4 %collective-permute-start.4 = (bf16[4,24,2048]{2,1,0:T(8,128)(2,1)S(1)}, bf16[4,24,2048]{2,1,0:T(8,128)(2,1)S(1)}, u32[]{:S(2)}, u32[]{:S(2)}) collective-permute-start(bf16[4,24,2048]{2,1,0:T(8,128)(2,1)S(1)} %fusion.73), channel_id=1, source_target_pairs={{0,3},{1,0},{2,1},{3,2},{4,7},{5,4},{6,5},{7,6},{8,11},{9,8},{10,9... | collective-permute-start | bytes 1179656 | tf_op jit(solution)/shard_map/ppermute | solution.py:35
  21.1 8.8 %collective-permute-done.4 = bf16[4,24,2048]{2,1,0:T(8,128)(2,1)S(1)} collective-permute-done((bf16[4,24,2048]{2,1,0:T(8,128)(2,1)S(1)}, bf16[4,24,2048]{2,1,0:T(8,128)(2,1)S(1)}, u32[]{:S(2)}, u32[]{:S(2)}) %collective-permute-start.4) | collective-permute-done | bytes 393248 | tf_op jit(solution)/shard_map/ppermute | solution.py:35
  30.0 22.1 %collective-permute-done.3 = bf16[4,24,2048]{2,1,0:T(8,128)(2,1)S(1)} collective-permute-done((bf16[4,24,2048]{2,1,0:T(8,128)(2,1)S(1)}, bf16[4,24,2048]{2,1,0:T(8,128)(2,1)S(1)}, u32[]{:S(2)}, u32[]{:S(2)}) %collective-permute-start.3) | collective-permute-done | bytes 393248 | tf_op jit(solution)/shard_map/ppermute | solution.py:35
  59.4 2.7 fusion.94
  68.7 3.8 %fusion.52 = bf16[4,24,32,32]{2,3,1,0:T(8,128)(2,1)} fusion(f32[4,24,32,32]{3,2,1,0:T(8,128)} %fusion.94, f32[4,24,64,32]{2,3,1,0:T(8,128)S(1)} %fusion.121, f32[4,24,64,32]{2,3,1,0:T(8,128)S(1)} %fusion.123, f32[32,64]{1,0:T(8,128)S(1)} %get-tuple-element.37, f32[32,64]{1,0:T(8,128)S(1)} %get-tuple-element.38, f32[64,64]{0,1:T(8,128)S(1)} %broadcast_multiply_fusion.2), kind=kOutput, calls=%fused_computation.70 | convolution fusion | flops 76283904 | bytes 3784704 | tf_op jit(solution)/shard_map/...kb,bm->...km/dot_general | solution.py:68
  76.5 3.5 %reshape.434 = bf16[64,2,1536]{2,1,0:T(2,128)(2,1)} reshape(bf16[1024,2,4,24]{3,2,1,0:T(4,128)(2,1)S(1)} %bitcast.289) | data formatting | bytes 786432
  80.0 13.7 %all-to-all-start = ((bf16[64,2,1536]{2,1,0:T(2,128)(2,1)}), bf16[64,2,1536]{2,1,0:T(2,128)(2,1)S(1)}, u32[]{:S(2)}, u32[]{:S(2)}) async-start(bf16[64,2,1536]{2,1,0:T(2,128)(2,1)} %reshape.434), calls=%async_computation | async-start | bytes 786432 | tf_op jit(solution)/shard_map/all_to_all | solution.py:166
  94.4 16.9 %all-to-all-done = bf16[64,2,1536]{2,1,0:T(2,128)(2,1)S(1)} async-done(((bf16[64,2,1536]{2,1,0:T(2,128)(2,1)}), bf16[64,2,1536]{2,1,0:T(2,128)(2,1)S(1)}, u32[]{:S(2)}, u32[]{:S(2)}) %all-to-all-start) | async-done | bytes 393248 | tf_op jit(solution)/shard_map/all_to_all | solution.py:166
  111.3 3.9 %reshape.435 = bf16[1024,2,4,24]{3,2,1,0:T(4,128)(2,1)} reshape(bf16[64,2,1536]{2,1,0:T(2,128)(2,1)S(1)} %all-to-all-done) | data formatting | bytes 786432
  115.3 5.5 %copy.352 = bf16[2,4,24,64,16]{4,3,2,1,0:T(8,128)(2,1)S(1)} copy(bf16[2,4,24,64,16]{2,1,0,4,3:T(4,128)(2,1)} %bitcast.291) | data formatting | bytes 786432 | tf_op jit(solution)/shard_map/all_to_all | solution.py:166
  120.7 2.8 fusion.336
  123.6 3.6 %copy.290 = bf16[1,64,4,24,16]{3,4,2,1,0:T(8,128)(2,1)S(1)} copy(bf16[1,64,4,24,16]{4,1,3,2,0:T(8,128)(2,1)} %get-tuple-element.11) | data formatting | bytes 393216 | tf_op jit(solution)/shard_map/slice | solution.py:167
  127.2 3.2 fusion.59
  132.3 4.1 %copy.294 = bf16[1,64,4,24,16]{3,4,2,1,0:T(8,128)(2,1)S(1)} copy(bf16[1,64,4,24,16]{4,1,3,2,0:T(8,128)(2,1)} %get-tuple-element.10) | data formatting | bytes 393216 | tf_op jit(solution)/shard_map/slice | solution.py:167
  145.9 3.9 %subtract_bitcast_fusion = f32[24,16,16,16]{0,2,3,1:T(8,128)} fusion(f32[24,16,16,16]{0,3,2,1:T(8,128)S(1)} %fusion.14, f32[24,16,16,16]{0,2,3,1:T(8,128)S(1)} %get-tuple-element.8), kind=kOutput, calls=%fused_computation.19 | convolution fusion | flops 18976256 | bytes 1179648 | tf_op jit(solution)/shard_map/...kb,bm->...km/dot_general | solution.py:68
  149.8 4.0 %add_bitcast_fusion = f32[24,16,16,16]{0,2,3,1:T(8,128)} fusion(f32[24,16,16,16]{0,3,2,1:T(8,128)S(1)} %fusion.12, f32[24,16,16,16]{0,2,3,1:T(8,128)S(1)} %get-tuple-element.8), kind=kOutput, calls=%fused_computation.18 | convolution fusion | flops 18976256 | bytes 1179648 | tf_op jit(solution)/shard_map/...kb,bm->...km/dot_general | solution.py:68
  153.8 3.8 %copy.307 = f32[24,16,16,16]{3,2,1,0:T(8,128)S(1)} copy(f32[24,16,16,16]{0,2,3,1:T(8,128)} %add_bitcast_fusion) | data formatting | bytes 786432 | tf_op jit(solution)/shard_map/add | solution.py:84
  159.1 3.8 %copy.304 = f32[24,16,16,16]{3,2,1,0:T(8,128)S(1)} copy(f32[24,16,16,16]{0,2,3,1:T(8,128)} %subtract_bitcast_fusion) | data formatting | bytes 786432 | tf_op jit(solution)/shard_map/sub | solution.py:80
  166.3 2.6 reshape.398
  169.0 3.4 copy.308
  172.4 3.3 fusion.153
  175.7 3.3 fusion.159
  179.0 2.6 reshape.399
  181.6 3.8 %copy.310 = f32[24,16,16,16]{0,2,3,1:T(8,128)S(1)} copy(f32[24,16,16,16]{3,2,1,0:T(8,128)} %reshape.399) | data formatting | bytes 786432 | tf_op jit(solution)/shard_map/reshape | solution.py:75
  185.4 3.8 %convolution_subtract_fusion = f32[24,16,16,16]{0,3,2,1:T(8,128)S(1)} fusion(f32[24,16,16,16]{0,3,2,1:T(8,128)} %fusion.159, f32[24,16,16,16]{0,2,3,1:T(8,128)S(1)} %copy.310), kind=kOutput, calls=%fused_computation.38 | convolution fusion | flops 18976256 | bytes 1179648 | tf_op jit(solution)/shard_map/ka,...ab->...kb/dot_general | solution.py:65
  189.2 2.6 fusion
  196.7 2.7 fusion.49
  199.4 3.6 %fusion.46 = bf16[24,16,16,16]{0,2,3,1:T(8,128)(2,1)} fusion(f32[24,16,16,16]{0,3,2,1:T(8,128)S(1)} %fusion.6, f32[24,16,16,16]{0,2,3,1:T(8,128)S(1)} %get-tuple-element.6), kind=kOutput, calls=%fused_computation.67 | convolution fusion | flops 19172864 | bytes 983040 | tf_op jit(solution)/shard_map/...kb,bm->...km/dot_general | solution.py:68
  203.0 3.9 %copy.318 = bf16[24,16,16,16]{3,2,1,0:T(8,128)(2,1)S(1)} copy(bf16[24,16,16,16]{0,2,3,1:T(8,128)(2,1)} %fusion.46) | data formatting | bytes 393216 | tf_op jit(solution)/shard_map/convert_element_type | solution.py:177
  208.4 2.7 copy.321
  212.7 3.1 copy.322
  215.8 3.5 %reshape.436 = bf16[64,2,1536]{2,1,0:T(2,128)(2,1)} reshape(bf16[256,2,16,24]{3,2,1,0:T(8,128)(2,1)S(1)} %bitcast.290) | data formatting | bytes 786432
  219.4 5.5 %all-to-all-start.1 = ((bf16[64,2,1536]{2,1,0:T(2,128)(2,1)}), bf16[64,2,1536]{2,1,0:T(2,128)(2,1)S(1)}, u32[]{:S(2)}, u32[]{:S(2)}) async-start(bf16[64,2,1536]{2,1,0:T(2,128)(2,1)} %reshape.436), calls=%async_computation.1 | async-start | bytes 786432 | tf_op jit(solution)/shard_map/all_to_all | solution.py:179
  230.4 9.6 %all-to-all-done.1 = bf16[64,2,1536]{2,1,0:T(2,128)(2,1)S(1)} async-done(((bf16[64,2,1536]{2,1,0:T(2,128)(2,1)}), bf16[64,2,1536]{2,1,0:T(2,128)(2,1)S(1)}, u32[]{:S(2)}, u32[]{:S(2)}) %all-to-all-start.1) | async-done | bytes 393248 | tf_op jit(solution)/shard_map/all_to_all | solution.py:179
  240.0 3.0 reshape.437
  243.0 2.6 copy.324
  253.9 3.3 reshape.403
  259.7 2.7 fusion.128
  266.9 3.0 convolution_add_fusion.2
  273.2 2.8 multiply_bitcast_fusion
  282.9 4.9 %gather_fusion = bf16[320,24]{1,0:T(8,128)(2,1)S(1)} fusion(bf16[4,24,2048]{1,2,0:T(8,128)(2,1)S(1)} %copy.330, s32[320]{0:T(512)S(1)} %fusion.233), kind=kCustom, calls=%fused_computation | custom fusion | bytes 33280 | tf_op jit(solution)/shard_map/gather | solution.py:200
  287.9 6.1 %collective-permute-start.6 = (bf16[320,24]{1,0:T(8,128)(2,1)S(1)}, bf16[320,24]{1,0:T(8,128)(2,1)S(1)}, u32[]{:S(2)}, u32[]{:S(2)}) collective-permute-start(bf16[320,24]{1,0:T(8,128)(2,1)S(1)} %gather_fusion), channel_id=1, source_target_pairs={{0,2},{1,3},{2,0},{3,1},{4,6},{5,7},{6,4},{7,5},{8,10},{9,11},{10,... | collective-permute-start | bytes 46088 | tf_op jit(solution)/shard_map/ppermute | solution.py:35
  296.1 2.6 collective-permute-done.6
  301.9 5.8 %all-to-all-start.2 = ((bf16[64,17,128]{2,1,0:T(8,128)(2,1)}), bf16[64,17,128]{2,1,0:T(8,128)(2,1)S(1)}, u32[]{:S(2)}, u32[]{:S(2)}) async-start(bf16[64,17,128]{2,1,0:T(8,128)(2,1)} %broadcast_in_dim.18), calls=%async_computation.2 | async-start | bytes 786432 | tf_op jit(solution)/shard_map/all_to_all | solution.py:215
  307.9 16.3 %all-to-all-done.2 = bf16[64,17,128]{2,1,0:T(8,128)(2,1)S(1)} async-done(((bf16[64,17,128]{2,1,0:T(8,128)(2,1)}), bf16[64,17,128]{2,1,0:T(8,128)(2,1)S(1)}, u32[]{:S(2)}, u32[]{:S(2)}) %all-to-all-start.2) | async-done | bytes 278560 | tf_op jit(solution)/shard_map/all_to_all | solution.py:215
  325.2 17.7 %all_to_all.40 = f32[64,16,2]{1,2,0:T(2,128)S(1)} all-to-all(f32[64,16,2]{1,2,0:T(2,128)S(1)} %copy.331), channel_id=1, replica_groups=mesh['rows'=64,'ch'=4] {'rows'}, dimensions={0} | all-to-all | bytes 16384 | tf_op jit(solution)/shard_map/all_to_all | solution.py:232
  (134 shorter events, 88.1 us)
Async XLA Ops:
  0.6 13.9 %copy-start.3 = (bf16[4,24,2048]{2,1,0:T(8,128)(2,1)S(1)}, bf16[4,24,2048]{2,1,0:T(8,128)(2,1)}, u32[]{:S(2)}) copy-start(bf16[4,24,2048]{2,1,0:T(8,128)(2,1)} %param.10) | copy-start | bytes 1179652
  1.7 7.4 %collective-permute-start = (bf16[2,24,2048]{2,1,0:T(8,128)(2,1)S(1)}, bf16[2,24,2048]{2,1,0:T(8,128)(2,1)S(1)}, u32[]{:S(2)}, u32[]{:S(2)}) collective-permute-start(bf16[2,24,2048]{2,1,0:T(8,128)(2,1)S(1)} %get-tuple-element.16), channel_id=1, source_target_pairs={{0,4},{4,8},{8,12},{12,16},{16,20},{20,24},{24,28},{28,32},{32,36}... | collective-permute-start | bytes 589832 | tf_op jit(solution)/shard_map/ppermute | solution.py:21
  6.2 7.0 %collective-permute-start.1 = (bf16[2,24,2048]{2,1,0:T(8,128)(2,1)S(1)}, bf16[2,24,2048]{2,1,0:T(8,128)(2,1)S(1)}, u32[]{:S(2)}, u32[]{:S(2)}) collective-permute-start(bf16[2,24,2048]{2,1,0:T(8,128)(2,1)S(1)} %get-tuple-element.17), channel_id=1, source_target_pairs={{4,0},{8,4},{12,8},{16,12},{20,16},{24,20},{28,24},{32,28},{36,32}... | collective-permute-start | bytes 589832 | tf_op jit(solution)/shard_map/ppermute | solution.py:23
  14.6 6.0 %copy-start.11 = (bf16[96,96]{1,0:T(8,128)(2,1)S(1)}, bf16[96,96]{1,0:T(8,128)(2,1)}, u32[]{:S(2)}) copy-start(bf16[96,96]{1,0:T(8,128)(2,1)} %param.12) | copy-start | bytes 55300
  15.6 14.4 %collective-permute-start.4 = (bf16[4,24,2048]{2,1,0:T(8,128)(2,1)S(1)}, bf16[4,24,2048]{2,1,0:T(8,128)(2,1)S(1)}, u32[]{:S(2)}, u32[]{:S(2)}) collective-permute-start(bf16[4,24,2048]{2,1,0:T(8,128)(2,1)S(1)} %fusion.73), channel_id=1, source_target_pairs={{0,3},{1,0},{2,1},{3,2},{4,7},{5,4},{6,5},{7,6},{8,11},{9,8},{10,9... | collective-permute-start | bytes 1179656 | tf_op jit(solution)/shard_map/ppermute | solution.py:35
  20.0 32.1 %collective-permute-start.3 = (bf16[4,24,2048]{2,1,0:T(8,128)(2,1)S(1)}, bf16[4,24,2048]{2,1,0:T(8,128)(2,1)S(1)}, u32[]{:S(2)}, u32[]{:S(2)}) collective-permute-start(bf16[4,24,2048]{2,1,0:T(8,128)(2,1)S(1)} %fusion.73), channel_id=1, source_target_pairs={{0,2},{1,3},{2,0},{3,1},{4,6},{5,7},{6,4},{7,5},{8,10},{9,11},{10,... | collective-permute-start | bytes 1179656 | tf_op jit(solution)/shard_map/ppermute | solution.py:35
  20.0 32.1 %collective-permute-start.2 = (bf16[4,24,2048]{2,1,0:T(8,128)(2,1)S(1)}, bf16[4,24,2048]{2,1,0:T(8,128)(2,1)S(1)}, u32[]{:S(2)}, u32[]{:S(2)}) collective-permute-start(bf16[4,24,2048]{2,1,0:T(8,128)(2,1)S(1)} %fusion.73), channel_id=1, source_target_pairs={{0,1},{1,2},{2,3},{3,0},{4,5},{5,6},{6,7},{7,4},{8,9},{9,10},{10,1... | collective-permute-start | bytes 1179656 | tf_op jit(solution)/shard_map/ppermute | solution.py:35
  52.6 0.8 copy-start.5
  54.1 0.9 copy-start.2
  76.5 17.2 %copy-start.12 = (bf16[24,128]{1,0:T(8,128)(2,1)S(1)}, bf16[24,128]{1,0:T(8,128)(2,1)}, u32[]{:S(2)}) copy-start(bf16[24,128]{1,0:T(8,128)(2,1)} %param.16) | copy-start | bytes 18436
  80.0 31.3 %all-to-all-start = ((bf16[64,2,1536]{2,1,0:T(2,128)(2,1)}), bf16[64,2,1536]{2,1,0:T(2,128)(2,1)S(1)}, u32[]{:S(2)}, u32[]{:S(2)}) async-start(bf16[64,2,1536]{2,1,0:T(2,128)(2,1)} %reshape.434), calls=%async_computation | async-start | bytes 786432 | tf_op jit(solution)/shard_map/all_to_all | solution.py:166
  136.5 2.0 copy-start.1
  185.4 3.8 %copy-start = (f32[24,16,16,16]{0,3,2,1:T(8,128)S(1)}, f32[24,16,16,16]{0,3,2,1:T(8,128)}, u32[]{:S(2)}) copy-start(f32[24,16,16,16]{0,3,2,1:T(8,128)} %fusion.153) | copy-start | bytes 1179652
  215.8 9.1 %copy-start.10 = (bf16[24,256]{1,0:T(8,128)(2,1)S(1)}, bf16[24,256]{1,0:T(8,128)(2,1)}, u32[]{:S(2)}) copy-start(bf16[24,256]{1,0:T(8,128)(2,1)} %constant_dynamic-update-slice_fusion.1) | copy-start | bytes 36868
  215.8 9.1 %copy-start.13 = (bf16[24,128]{1,0:T(8,128)(2,1)S(1)}, bf16[24,128]{1,0:T(8,128)(2,1)}, u32[]{:S(2)}) copy-start(bf16[24,128]{1,0:T(8,128)(2,1)} %param.15) | copy-start | bytes 18436
  215.8 12.6 %copy-start.14 = (s32[256]{0:T(256)S(1)}, s32[256]{0:T(256)}, u32[]{:S(2)}) copy-start(s32[256]{0:T(256)} %param.18) | copy-start | bytes 3076
  215.8 12.6 %copy-start.15 = (s32[64]{0:T(128)S(1)}, s32[64]{0:T(128)}, u32[]{:S(2)}) copy-start(s32[64]{0:T(128)} %param.17) | copy-start | bytes 772
  215.8 12.6 %copy-start.16 = (s32[64]{0:T(128)S(1)}, s32[64]{0:T(128)}, u32[]{:S(2)}) copy-start(s32[64]{0:T(128)} %param.19) | copy-start | bytes 772
  219.4 20.7 %all-to-all-start.1 = ((bf16[64,2,1536]{2,1,0:T(2,128)(2,1)}), bf16[64,2,1536]{2,1,0:T(2,128)(2,1)S(1)}, u32[]{:S(2)}, u32[]{:S(2)}) async-start(bf16[64,2,1536]{2,1,0:T(2,128)(2,1)} %reshape.436), calls=%async_computation.1 | async-start | bytes 786432 | tf_op jit(solution)/shard_map/all_to_all | solution.py:179
  224.9 69.1 %collective-permute-start.10 = (bf16[24,256]{1,0:T(8,128)(2,1)S(1)}, bf16[24,256]{1,0:T(8,128)(2,1)}, u32[]{:S(2)}, u32[]{:S(2)}) collective-permute-start(bf16[24,256]{1,0:T(8,128)(2,1)S(1)} %constant_dynamic-update-slice_fusion), channel_id=1, source_target_pairs={{0,3},{1,0},{2,1},{3,2},{4,7},{5,4},{6,5},{7,6},{8,11},{9,8},{10,9... | collective-permute-start | bytes 36872 | tf_op jit(solution)/shard_map/ppermute | solution.py:35
  225.0 70.4 %collective-permute-start.9 = (bf16[24,256]{1,0:T(8,128)(2,1)S(1)}, bf16[24,256]{1,0:T(8,128)(2,1)}, u32[]{:S(2)}, u32[]{:S(2)}) collective-permute-start(bf16[24,256]{1,0:T(8,128)(2,1)S(1)} %constant_dynamic-update-slice_fusion), channel_id=1, source_target_pairs={{0,2},{1,3},{2,0},{3,1},{4,6},{5,7},{6,4},{7,5},{8,10},{9,11},{10,... | collective-permute-start | bytes 36872 | tf_op jit(solution)/shard_map/ppermute | solution.py:35
  227.1 68.3 %collective-permute-start.8 = (bf16[24,256]{1,0:T(8,128)(2,1)S(1)}, bf16[24,256]{1,0:T(8,128)(2,1)}, u32[]{:S(2)}, u32[]{:S(2)}) collective-permute-start(bf16[24,256]{1,0:T(8,128)(2,1)S(1)} %constant_dynamic-update-slice_fusion), channel_id=1, source_target_pairs={{0,1},{1,2},{2,3},{3,0},{4,5},{5,6},{6,7},{7,4},{8,9},{9,10},{10,1... | collective-permute-start | bytes 36872 | tf_op jit(solution)/shard_map/ppermute | solution.py:35
  262.4 1.6 copy-start.7
  270.0 1.6 copy-start.8
  270.0 1.6 copy-start.9
  278.2 2.4 copy-start.6
  281.8 20.2 %copy-start.4 = (bf16[4,24,2048]{2,1,0:T(8,128)(2,1)}, bf16[4,24,2048]{2,1,0:T(8,128)(2,1)S(1)}, u32[]{:S(2)}) copy-start(bf16[4,24,2048]{2,1,0:T(8,128)(2,1)S(1)} %add_convert_fusion.1) | copy-start | bytes 1179652
  281.8 19.3 %copy-start.17 = (bf16[1,128]{1,0:T(2,128)(2,1)S(1)}, bf16[1,128]{1,0:T(2,128)(2,1)}, u32[]{:S(2)}) copy-start(bf16[1,128]{1,0:T(2,128)(2,1)} %fusion.236) | copy-start | bytes 772
  287.8 8.3 %collective-permute-start.7 = (bf16[320,24]{1,0:T(8,128)(2,1)S(1)}, bf16[320,24]{1,0:T(8,128)(2,1)S(1)}, u32[]{:S(2)}, u32[]{:S(2)}) collective-permute-start(bf16[320,24]{1,0:T(8,128)(2,1)S(1)} %gather_fusion), channel_id=1, source_target_pairs={{0,3},{1,0},{2,1},{3,2},{4,7},{5,4},{6,5},{7,6},{8,11},{9,8},{10,9... | collective-permute-start | bytes 46088 | tf_op jit(solution)/shard_map/ppermute | solution.py:35
  287.9 10.9 %collective-permute-start.6 = (bf16[320,24]{1,0:T(8,128)(2,1)S(1)}, bf16[320,24]{1,0:T(8,128)(2,1)S(1)}, u32[]{:S(2)}, u32[]{:S(2)}) collective-permute-start(bf16[320,24]{1,0:T(8,128)(2,1)S(1)} %gather_fusion), channel_id=1, source_target_pairs={{0,2},{1,3},{2,0},{3,1},{4,6},{5,7},{6,4},{7,5},{8,10},{9,11},{10,... | collective-permute-start | bytes 46088 | tf_op jit(solution)/shard_map/ppermute | solution.py:35
  294.0 6.6 %collective-permute-start.5 = (bf16[320,24]{1,0:T(8,128)(2,1)S(1)}, bf16[320,24]{1,0:T(8,128)(2,1)S(1)}, u32[]{:S(2)}, u32[]{:S(2)}) collective-permute-start(bf16[320,24]{1,0:T(8,128)(2,1)S(1)} %gather_fusion), channel_id=1, source_target_pairs={{0,1},{1,2},{2,3},{3,0},{4,5},{5,6},{6,7},{7,4},{8,9},{9,10},{10,1... | collective-permute-start | bytes 46088 | tf_op jit(solution)/shard_map/ppermute | solution.py:35
  301.9 22.3 %all-to-all-start.2 = ((bf16[64,17,128]{2,1,0:T(8,128)(2,1)}), bf16[64,17,128]{2,1,0:T(8,128)(2,1)S(1)}, u32[]{:S(2)}, u32[]{:S(2)}) async-start(bf16[64,17,128]{2,1,0:T(8,128)(2,1)} %broadcast_in_dim.18), calls=%async_computation.2 | async-start | bytes 786432 | tf_op jit(solution)/shard_map/all_to_all | solution.py:215
